TPU v7x, 512 devices: a whole 4x4x16 slice. The times are simulated.
512 devices in a mesh: dom: 64 (over z, y), rep: 8 (over x, core).
Axes of the slice: x: 4, y: 4, z: 16, core: 2. Of those that a mesh axis runs over, the one named last changes fastest.
Arguments:
- feats: bfloat16 [65536, 128], P(('dom', 'rep')), may hold values from -6 to 6
- weight: bfloat16 [128, 128], replicated, may hold values from -0.5 to 0.5
- bias: float32 [128], replicated, may hold values from -3 to 3
- tiles: bfloat16 [512, 5, 28, 128, 128], P(('dom', 'rep')), may hold values from -0.0625 to 0.0625
- tile_cols: int32 [512, 5, 28], P(('dom', 'rep')), may hold values from 0 to 7
- tile_count: int32 [512, 5], P(('dom', 'rep')), may hold values from 2 to 28, as said below
- cotangent: bfloat16 [65536, 128], P(('dom', 'rep')), may hold values from -6 to 6
Outputs:
- hidden: bfloat16 [65536, 128], P(('dom', 'rep'))
- grad_weight: float32 [128, 128], replicated
- grad_bias: float32 [128], replicated
- grad_feats: bfloat16 [65536, 128], P(('dom', 'rep'))
Inputs may be any that keep to these rules, and one draw needn't show every extreme that they name: `tile_count`: every list has at least two live tiles; the nodes of some device have 28 live tiles in every list, and those of most devices far fewer.
All inputs are finite; a program needn't handle non-finite values.
Results may differ from a plain program's by a relative error of at most 0.0062.
Values may be sent and summed in bfloat16 or wider, within the bound.
A program may use at most 64 MiB of HBM per device.

v0:
```python
import jax
import jax.numpy as jnp
from jax import lax
from jax.sharding import PartitionSpec as P


def swapped(value, axis, bit):
    mask = 2**bit
    pairs = [(source, source ^ mask) for source in range(lax.axis_size(axis))]
    return lax.ppermute(value, axis, pairs)


def gelu_tanh(values):
    return jax.nn.gelu(values, approximate=True)


def add_slot(summed, panel, slot, tiles, tile_cols, live_mask):
    tgt_blocks, slot_count, max_tiles, block, unused = tiles.shape
    width = panel.shape[1]
    panel_blocks = panel.shape[0] // block
    source = panel.reshape(panel_blocks, block, width)
    columns = tile_cols[:, slot]
    slot_tiles = tiles[:, slot]
    fetched = source[columns]
    fetched = jnp.where(live_mask[:, slot][:, :, None, None], fetched, jnp.zeros((), jnp.bfloat16))
    return summed + jnp.einsum(
        "tmij,tmjh->tih", slot_tiles, fetched, preferred_element_type=jnp.float32
    )


def partial_panel(slot, tiles, tile_cols, live_mask, grad_rows_b, panel_blocks):
    tgt_blocks, slot_count, max_tiles, block, unused = tiles.shape
    width = grad_rows_b.shape[2]
    masked = jnp.where(
        live_mask[:, slot][:, :, None, None], tiles[:, slot], jnp.zeros((), jnp.bfloat16)
    )
    contrib = jnp.einsum("tmij,tih->tmjh", masked, grad_rows_b, preferred_element_type=jnp.float32)
    targets = tile_cols[:, slot].reshape(tgt_blocks * max_tiles)
    placed = jnp.zeros((panel_blocks, block, width), jnp.float32)
    placed = placed.at[targets].add(contrib.reshape(tgt_blocks * max_tiles, block, width))
    return placed.reshape(panel_blocks * block, width)


def body(feats, weight, bias, tiles, tile_cols, tile_count, cotangent):
    dom_size = lax.axis_size("dom")
    rep_size = lax.axis_size("rep")
    top_bit = dom_size.bit_length() - 1
    tgt_blocks, slot_count, max_tiles, block, unused = tiles.shape
    width = weight.shape[1]
    panel_blocks = rep_size * tgt_blocks
    live_mask = jnp.arange(max_tiles)[None, None, :] < tile_count[:, :, None]
    projected = jnp.dot(feats, weight, preferred_element_type=jnp.float32).astype(jnp.bfloat16)
    own_rows = lax.all_gather(projected, "rep", axis=0, tiled=True)
    summed = jnp.zeros((tgt_blocks, block, width), jnp.float32)
    summed = add_slot(summed, own_rows, 0, tiles, tile_cols, live_mask)
    for round_index in range(1, slot_count):
        bit_number = top_bit - round_index
        partner_rows = swapped(own_rows, "dom", bit_number)
        summed = add_slot(summed, partner_rows, round_index, tiles, tile_cols, live_mask)
    preact = summed.reshape(tgt_blocks * block, width) + bias
    hidden_f, pullback = jax.vjp(gelu_tanh, preact)
    hidden = hidden_f.astype(jnp.bfloat16)
    grad_pre = pullback(cotangent.astype(jnp.float32))[0]
    grad_rows_b = grad_pre.astype(jnp.bfloat16).reshape(tgt_blocks, block, width)
    grad_panel = partial_panel(0, tiles, tile_cols, live_mask, grad_rows_b, panel_blocks)
    for round_index in range(1, slot_count):
        outgoing = partial_panel(
            round_index, tiles, tile_cols, live_mask, grad_rows_b, panel_blocks
        )
        grad_panel = grad_panel + swapped(outgoing, "dom", top_bit - round_index)
    grad_proj = lax.psum_scatter(grad_panel, "rep", scatter_dimension=0, tiled=True).astype(
        jnp.bfloat16
    )
    weight_local = lax.dot_general(
        feats, grad_proj, (((0,), (0,)), ((), ())), preferred_element_type=jnp.float32
    )
    bias_local = jnp.sum(grad_pre, axis=0)
    grad_weight, grad_bias = lax.psum((weight_local, bias_local), ("dom", "rep"))
    grad_feats = lax.dot_general(
        grad_proj, weight, (((1,), (1,)), ((), ())), preferred_element_type=jnp.float32
    ).astype(jnp.bfloat16)
    return (hidden, grad_weight, grad_bias, grad_feats)


def solution(mesh):
    return jax.shard_map(
        body,
        mesh=mesh,
        in_specs=(
            P(("dom", "rep"), None),
            P(),
            P(),
            P(("dom", "rep"), None, None, None, None),
            P(("dom", "rep"), None, None),
            P(("dom", "rep"), None),
            P(("dom", "rep"), None),
        ),
        out_specs=(P(("dom", "rep"), None), P(), P(), P(("dom", "rep"), None)),
        check_vma=False,
    )
```

profile of v0, /device:TPU:1, one launch (start us, length us, event | category | flops | bytes accessed | tf_op | source)
XLA Modules:
  0.0 770.6 jit_solution(12770402989602264046)
XLA Ops:
  8.8 19.5 %all_gather.3 = bf16[1024,128]{1,0:T(8,128)(2,1)S(1)} all-gather(bf16[128,128]{1,0:T(8,128)(2,1)S(1)} %convolution_convert_fusion.1), channel_id=1, replica_groups=mesh['dom'=64,'rep'=8] {'rep'}, dimensions={0}, use_global_device_ids=true | all-gather | bytes 294912 | tf_op jit(solution)/shard_map/all_gather | solution.py:53
  28.3 1.9 collective-permute-start.3
  30.2 1.9 collective-permute-start.2
  32.2 8.4 %collective-permute-start.1 = (bf16[1024,128]{1,0:T(8,128)(2,1)S(1)}, bf16[1024,128]{1,0:T(8,128)(2,1)S(1)}, u32[]{:S(2)}, u32[]{:S(2)}) collective-permute-start(bf16[1024,128]{1,0:T(8,128)(2,1)S(1)} %all_gather.3), channel_id=1, source_target_pairs={{0,128},{8,136},{16,144},{24,152},{32,160},{40,168},{48,176},{56,1... | collective-permute-start | bytes 786440 | tf_op jit(solution)/shard_map/ppermute | solution.py:10
  40.6 7.9 %collective-permute-start = (bf16[1024,128]{1,0:T(8,128)(2,1)S(1)}, bf16[1024,128]{1,0:T(8,128)(2,1)S(1)}, u32[]{:S(2)}, u32[]{:S(2)}) collective-permute-start(bf16[1024,128]{1,0:T(8,128)(2,1)S(1)} %all_gather.3), channel_id=1, source_target_pairs={{0,256},{8,264},{16,272},{24,280},{32,288},{40,296},{48,304},{56,3... | collective-permute-start | bytes 786440 | tf_op jit(solution)/shard_map/ppermute | solution.py:10
  51.5 1.6 convolution_bitcast_fusion.4
  53.9 1.6 convolution_bitcast_fusion
  55.6 8.0 %collective-permute-done.2 = bf16[1024,128]{1,0:T(8,128)(2,1)S(1)} collective-permute-done((bf16[1024,128]{1,0:T(8,128)(2,1)S(1)}, bf16[1024,128]{1,0:T(8,128)(2,1)S(1)}, u32[]{:S(2)}, u32[]{:S(2)}) %collective-permute-start.2) | collective-permute-done | bytes 262176 | tf_op jit(solution)/shard_map/ppermute | solution.py:10
  64.3 1.6 convolution_bitcast_fusion.1
  66.0 19.9 %collective-permute-done.1 = bf16[1024,128]{1,0:T(8,128)(2,1)S(1)} collective-permute-done((bf16[1024,128]{1,0:T(8,128)(2,1)S(1)}, bf16[1024,128]{1,0:T(8,128)(2,1)S(1)}, u32[]{:S(2)}, u32[]{:S(2)}) %collective-permute-start.1) | collective-permute-done | bytes 262176 | tf_op jit(solution)/shard_map/ppermute | solution.py:10
  86.7 1.6 convolution_bitcast_fusion.2
  89.1 2.3 fusion.100
  91.4 3.2 fusion.12
  94.6 3.2 fusion.10
  97.8 2.0 fusion.8
  99.8 3.2 fusion.6
  103.0 4.6 scatter_fusion.1
  107.6 11.3 %collective-permute-start.4 = (f32[1024,128]{1,0:T(8,128)S(1)}, f32[1024,128]{1,0:T(8,128)}, u32[]{:S(2)}, u32[]{:S(2)}) collective-permute-start(f32[1024,128]{1,0:T(8,128)S(1)} %bitcast.141), channel_id=1, source_target_pairs={{0,256},{8,264},{16,272},{24,280},{32,288},{40,296},{48,304},{56,3... | collective-permute-start | bytes 1572872 | tf_op jit(solution)/shard_map/ppermute | solution.py:10
  118.9 4.6 scatter_fusion.2
  123.5 1.9 collective-permute-start.5
  125.5 2.6 scatter_fusion.3
  128.1 1.9 collective-permute-start.6
  130.1 4.6 scatter_fusion.4
  134.7 1.9 collective-permute-start.7
  136.6 3.2 fusion.14
  139.9 4.6 scatter_fusion
  144.5 8.2 %collective-permute-done.4 = f32[1024,128]{1,0:T(8,128)} collective-permute-done((f32[1024,128]{1,0:T(8,128)S(1)}, f32[1024,128]{1,0:T(8,128)}, u32[]{:S(2)}, u32[]{:S(2)}) %collective-permute-start.4) | collective-permute-done | bytes 524320 | tf_op jit(solution)/shard_map/ppermute | solution.py:10
  152.6 51.6 %collective-permute-done.5 = f32[1024,128]{1,0:T(8,128)} collective-permute-done((f32[1024,128]{1,0:T(8,128)S(1)}, f32[1024,128]{1,0:T(8,128)}, u32[]{:S(2)}, u32[]{:S(2)}) %collective-permute-start.5) | collective-permute-done | bytes 524320 | tf_op jit(solution)/shard_map/ppermute | solution.py:10
  204.2 2.3 fusion.53
  206.5 114.1 %psum.15 = f32[128]{0:T(128)} all-reduce(f32[128]{0:T(128)S(1)} %get-tuple-element.8), channel_id=1, replica_groups=mesh['dom'=64,'rep'=8] {'dom','rep'}, use_global_device_ids=true, to_apply=%region_8.9 | all-reduce | flops 128 | bytes 1024 | tf_op jit(solution)/shard_map/psum | solution.py:78
  320.7 1.7 convolution_bitcast_fusion.5
  324.0 438.2 %all-reduce.2.cloned.1.call-done = f32[128,128]{0,1:T(8,128)} async-done(((f32[128,128]{0,1:T(8,128)}), f32[128,128]{0,1:T(8,128)}) %all-reduce.2.cloned.1.call-update) | async-done | bytes 65552 | tf_op jit(solution)/shard_map/psum | solution.py:78
  (39 shorter events, 10.9 us)
Async XLA Ops:
  7.2 0.8 copy-start
  7.2 313.5 %reduce-scatter.2.cloned.1.call-start = ((), (), s32[]{:S(2)}) async-start(), calls=%async_computation.1 | async-start | bytes 589824 | tf_op jit(solution)/shard_map/reduce_scatter | solution.py:71
  28.3 24.9 %collective-permute-start.3 = (bf16[1024,128]{1,0:T(8,128)(2,1)S(1)}, bf16[1024,128]{1,0:T(8,128)(2,1)S(1)}, u32[]{:S(2)}, u32[]{:S(2)}) collective-permute-start(bf16[1024,128]{1,0:T(8,128)(2,1)S(1)} %all_gather.3), channel_id=1, source_target_pairs={{0,32},{8,40},{16,48},{24,56},{32,0},{40,8},{48,16},{56,24},{64,96... | collective-permute-start | bytes 786440 | tf_op jit(solution)/shard_map/ppermute | solution.py:10
  30.2 33.4 %collective-permute-start.2 = (bf16[1024,128]{1,0:T(8,128)(2,1)S(1)}, bf16[1024,128]{1,0:T(8,128)(2,1)S(1)}, u32[]{:S(2)}, u32[]{:S(2)}) collective-permute-start(bf16[1024,128]{1,0:T(8,128)(2,1)S(1)} %all_gather.3), channel_id=1, source_target_pairs={{0,64},{8,72},{16,80},{24,88},{32,96},{40,104},{48,112},{56,120},{... | collective-permute-start | bytes 786440 | tf_op jit(solution)/shard_map/ppermute | solution.py:10
  32.2 53.7 %collective-permute-start.1 = (bf16[1024,128]{1,0:T(8,128)(2,1)S(1)}, bf16[1024,128]{1,0:T(8,128)(2,1)S(1)}, u32[]{:S(2)}, u32[]{:S(2)}) collective-permute-start(bf16[1024,128]{1,0:T(8,128)(2,1)S(1)} %all_gather.3), channel_id=1, source_target_pairs={{0,128},{8,136},{16,144},{24,152},{32,160},{40,168},{48,176},{56,1... | collective-permute-start | bytes 786440 | tf_op jit(solution)/shard_map/ppermute | solution.py:10
  40.6 47.7 %collective-permute-start = (bf16[1024,128]{1,0:T(8,128)(2,1)S(1)}, bf16[1024,128]{1,0:T(8,128)(2,1)S(1)}, u32[]{:S(2)}, u32[]{:S(2)}) collective-permute-start(bf16[1024,128]{1,0:T(8,128)(2,1)S(1)} %all_gather.3), channel_id=1, source_target_pairs={{0,256},{8,264},{16,272},{24,280},{32,288},{40,296},{48,304},{56,3... | collective-permute-start | bytes 786440 | tf_op jit(solution)/shard_map/ppermute | solution.py:10
  86.6 2.4 copy-start.2
  86.6 2.4 copy-start.3
  107.6 45.0 %collective-permute-start.4 = (f32[1024,128]{1,0:T(8,128)S(1)}, f32[1024,128]{1,0:T(8,128)}, u32[]{:S(2)}, u32[]{:S(2)}) collective-permute-start(f32[1024,128]{1,0:T(8,128)S(1)} %bitcast.141), channel_id=1, source_target_pairs={{0,256},{8,264},{16,272},{24,280},{32,288},{40,296},{48,304},{56,3... | collective-permute-start | bytes 1572872 | tf_op jit(solution)/shard_map/ppermute | solution.py:10
  123.5 80.7 %collective-permute-start.5 = (f32[1024,128]{1,0:T(8,128)S(1)}, f32[1024,128]{1,0:T(8,128)}, u32[]{:S(2)}, u32[]{:S(2)}) collective-permute-start(f32[1024,128]{1,0:T(8,128)S(1)} %bitcast.142), channel_id=1, source_target_pairs={{0,128},{8,136},{16,144},{24,152},{32,160},{40,168},{48,176},{56,1... | collective-permute-start | bytes 1572872 | tf_op jit(solution)/shard_map/ppermute | solution.py:10
  128.1 76.1 %collective-permute-start.6 = (f32[1024,128]{1,0:T(8,128)S(1)}, f32[1024,128]{1,0:T(8,128)S(1)}, u32[]{:S(2)}, u32[]{:S(2)}) collective-permute-start(f32[1024,128]{1,0:T(8,128)S(1)} %bitcast.143), channel_id=1, source_target_pairs={{0,64},{8,72},{16,80},{24,88},{32,96},{40,104},{48,112},{56,120},{... | collective-permute-start | bytes 1572872 | tf_op jit(solution)/shard_map/ppermute | solution.py:10
  134.7 69.5 %collective-permute-start.7 = (f32[1024,128]{1,0:T(8,128)S(1)}, f32[1024,128]{1,0:T(8,128)}, u32[]{:S(2)}, u32[]{:S(2)}) collective-permute-start(f32[1024,128]{1,0:T(8,128)S(1)} %bitcast.144), channel_id=1, source_target_pairs={{0,32},{8,40},{16,48},{24,56},{32,0},{40,8},{48,16},{56,24},{64,96... | collective-permute-start | bytes 1572872 | tf_op jit(solution)/shard_map/ppermute | solution.py:10
  144.4 177.9 %copy-start.1 = (bf16[128,128]{1,0:T(8,128)(2,1)S(1)}, bf16[128,128]{1,0:T(8,128)(2,1)}, u32[]{:S(2)}) copy-start(bf16[128,128]{1,0:T(8,128)(2,1)} %param.8) | copy-start | bytes 98308
  206.5 555.7 %all-reduce.2.cloned.1.call-start = ((), (), s32[]{:S(2)}) async-start(), calls=%async_computation.2 | async-start | bytes 131072 | tf_op jit(solution)/shard_map/psum | solution.py:78
Sparse Core Ops, SparseCore 0:
  206.6 44.0 reduce-scatter.1
  322.5 439.6 all-reduce.1
where the time goes:
time: 772 us; the launch traced here: 771 us
  waiting for transfers between devices  526 us (68%)
  blocking collectives  134 us (17%)
  starting transfers between devices  37.3 us (5%)
  matrix products  27.8 us (4%)
  other arithmetic  25.4 us (3%)
  between operations  14.3 us (2%)
    psum x1, waiting for transfers between devices, body(): lax.psum((weight_local, bias_local), ('dom', 'rep'))  438 us
    psum x1, blocking collectives, body(): lax.psum((weight_local, bias_local), ('dom', 'rep'))  114 us
    ppermute x8, waiting for transfers between devices, swapped(): return lax.ppermute(value, axis, pairs)  87.7 us
    ppermute x8, starting transfers between devices, swapped(): return lax.ppermute(value, axis, pairs)  37.2 us
    scatter-add x5, other arithmetic, partial_panel(): placed.at[targets]  20.9 us
    all_gather x1, blocking collectives, body(): own_rows = lax.all_gather(projected, 'rep', axis=0, tiled=True)  19.5 us
  transfers between devices with their start and end apart: 10, of which 5 were waited for; matrix products, arithmetic and copies ran while one was open for 4% of the time, Pallas kernels for 0%

commit v1 on v0

--- a/solution.py
+++ b/solution.py
@@ -75,7 +75,7 @@
         feats, grad_proj, (((0,), (0,)), ((), ())), preferred_element_type=jnp.float32
     )
     bias_local = jnp.sum(grad_pre, axis=0)
-    grad_weight, grad_bias = lax.psum((weight_local, bias_local), ("dom", "rep"))
+    grad_weight, grad_bias = lax.psum(lax.psum((weight_local, bias_local), "rep"), "dom")
     grad_feats = lax.dot_general(
         grad_proj, weight, (((1,), (1,)), ((), ())), preferred_element_type=jnp.float32
     ).astype(jnp.bfloat16)

time: 772 us -> 676 us (0.88); the launches traced: 771 us -> 664 us
  waiting for transfers between devices: 526 us -> 402 us
  blocking collectives: 134 us -> 151 us
    psum x1 -> x2, waiting for transfers between devices: 438 us -> 270 us  [the longest x1 270 us: body(): lax.psum(lax.psum((weight_local, bias_local), 'rep'), 'dom')]
    reduce_scatter x1, waiting for transfers between devices: 0.01 us -> 44.2 us  [body(): lax.psum_scatter(grad_panel, 'rep', scatter_dimension=0, tiled=True)]
    psum x1 -> x2, blocking collectives: 114 us -> 131 us  [the longest x1 117 us: body(): lax.psum(lax.psum((weight_local, bias_local), 'rep'), 'dom')]
  transfers between devices with their start and end apart: 10 -> 11, of which waited for: 5 -> 6; matrix products, arithmetic and copies ran while one was open for 4% -> 5% of each run, Pallas kernels for 0% -> 0%
where the time goes in v1:
time: 676 us; the launch traced here: 664 us
  waiting for transfers between devices  402 us (59%)
  blocking collectives  151 us (22%)
  starting transfers between devices  37.4 us (6%)
  matrix products  27.8 us (4%)
  other arithmetic  25.4 us (4%)
  between operations  14 us (2%)
    psum x1, waiting for transfers between devices, body(): lax.psum(lax.psum((weight_local, bias_local), 'rep'), 'dom')  270 us
    psum x1, blocking collectives, body(): lax.psum(lax.psum((weight_local, bias_local), 'rep'), 'dom')  117 us
    ppermute x8, waiting for transfers between devices, swapped(): return lax.ppermute(value, axis, pairs)  87.7 us
    reduce_scatter x1, waiting for transfers between devices, body(): lax.psum_scatter(grad_panel, 'rep', scatter_dimension=0, tiled=True)  44.2 us
    ppermute x8, starting transfers between devices, swapped(): return lax.ppermute(value, axis, pairs)  37.2 us
    scatter-add x5, other arithmetic, partial_panel(): placed.at[targets]  20.9 us
    all_gather x1, blocking collectives, body(): own_rows = lax.all_gather(projected, 'rep', axis=0, tiled=True)  19.5 us
    dot_general x5, matrix products, partial_panel(): jnp.einsum('tmij,tih->tmjh', masked, grad_rows_b, preferred_element_type=...  14.8 us
  transfers between devices with their start and end apart: 11, of which 6 were waited for; matrix products, arithmetic and copies ran while one was open for 5% of the time, Pallas kernels for 0%

profile of v1, /device:TPU:1, one launch (start us, length us, event | category | flops | bytes accessed | tf_op | source)
XLA Modules:
  0.0 663.9 jit_solution(14139815691807882995)
XLA Ops:
  8.8 19.5 %all_gather.3 = bf16[1024,128]{1,0:T(8,128)(2,1)S(1)} all-gather(bf16[128,128]{1,0:T(8,128)(2,1)S(1)} %convolution_convert_fusion.1), channel_id=1, replica_groups=mesh['dom'=64,'rep'=8] {'rep'}, dimensions={0}, use_global_device_ids=true | all-gather | bytes 294912 | tf_op jit(solution)/shard_map/all_gather | solution.py:53
  28.3 1.9 collective-permute-start.3
  30.2 1.9 collective-permute-start.2
  32.2 8.4 %collective-permute-start.1 = (bf16[1024,128]{1,0:T(8,128)(2,1)S(1)}, bf16[1024,128]{1,0:T(8,128)(2,1)S(1)}, u32[]{:S(2)}, u32[]{:S(2)}) collective-permute-start(bf16[1024,128]{1,0:T(8,128)(2,1)S(1)} %all_gather.3), channel_id=1, source_target_pairs={{0,128},{8,136},{16,144},{24,152},{32,160},{40,168},{48,176},{56,1... | collective-permute-start | bytes 786440 | tf_op jit(solution)/shard_map/ppermute | solution.py:10
  40.6 7.9 %collective-permute-start = (bf16[1024,128]{1,0:T(8,128)(2,1)S(1)}, bf16[1024,128]{1,0:T(8,128)(2,1)S(1)}, u32[]{:S(2)}, u32[]{:S(2)}) collective-permute-start(bf16[1024,128]{1,0:T(8,128)(2,1)S(1)} %all_gather.3), channel_id=1, source_target_pairs={{0,256},{8,264},{16,272},{24,280},{32,288},{40,296},{48,304},{56,3... | collective-permute-start | bytes 786440 | tf_op jit(solution)/shard_map/ppermute | solution.py:10
  55.6 8.0 %collective-permute-done.2 = bf16[1024,128]{1,0:T(8,128)(2,1)S(1)} collective-permute-done((bf16[1024,128]{1,0:T(8,128)(2,1)S(1)}, bf16[1024,128]{1,0:T(8,128)(2,1)S(1)}, u32[]{:S(2)}, u32[]{:S(2)}) %collective-permute-start.2) | collective-permute-done | bytes 262176 | tf_op jit(solution)/shard_map/ppermute | solution.py:10
  64.3 1.6 convolution_bitcast_fusion.1
  66.0 19.9 %collective-permute-done.1 = bf16[1024,128]{1,0:T(8,128)(2,1)S(1)} collective-permute-done((bf16[1024,128]{1,0:T(8,128)(2,1)S(1)}, bf16[1024,128]{1,0:T(8,128)(2,1)S(1)}, u32[]{:S(2)}, u32[]{:S(2)}) %collective-permute-start.1) | collective-permute-done | bytes 262176 | tf_op jit(solution)/shard_map/ppermute | solution.py:10
  86.7 1.6 convolution_bitcast_fusion.2
  89.1 2.3 fusion.100
  91.4 3.2 fusion.12
  94.6 3.2 fusion.10
  97.8 2.0 fusion.8
  99.8 3.2 fusion.6
  103.0 4.6 scatter_fusion.1
  107.6 11.3 %collective-permute-start.4 = (f32[1024,128]{1,0:T(8,128)S(1)}, f32[1024,128]{1,0:T(8,128)}, u32[]{:S(2)}, u32[]{:S(2)}) collective-permute-start(f32[1024,128]{1,0:T(8,128)S(1)} %bitcast.141), channel_id=1, source_target_pairs={{0,256},{8,264},{16,272},{24,280},{32,288},{40,296},{48,304},{56,3... | collective-permute-start | bytes 1572872 | tf_op jit(solution)/shard_map/ppermute | solution.py:10
  118.9 4.6 scatter_fusion.2
  123.5 1.9 collective-permute-start.5
  125.5 2.6 scatter_fusion.3
  128.1 1.9 collective-permute-start.6
  130.1 4.6 scatter_fusion.4
  134.7 1.9 collective-permute-start.7
  136.6 3.2 fusion.14
  139.9 4.6 scatter_fusion
  144.5 8.2 %collective-permute-done.4 = f32[1024,128]{1,0:T(8,128)} collective-permute-done((f32[1024,128]{1,0:T(8,128)S(1)}, f32[1024,128]{1,0:T(8,128)}, u32[]{:S(2)}, u32[]{:S(2)}) %collective-permute-start.4) | collective-permute-done | bytes 524320 | tf_op jit(solution)/shard_map/ppermute | solution.py:10
  152.6 51.6 %collective-permute-done.5 = f32[1024,128]{1,0:T(8,128)} collective-permute-done((f32[1024,128]{1,0:T(8,128)S(1)}, f32[1024,128]{1,0:T(8,128)}, u32[]{:S(2)}, u32[]{:S(2)}) %collective-permute-start.5) | collective-permute-done | bytes 524320 | tf_op jit(solution)/shard_map/ppermute | solution.py:10
  204.2 2.3 fusion.53
  206.5 44.2 %reduce-scatter.2.cloned.1.call-done = f32[128,128]{1,0:T(8,128)} async-done(((f32[1024,128]{1,0:T(8,128)}), f32[128,128]{1,0:T(8,128)}) %reduce-scatter.2.cloned.1.call-update) | async-done | bytes 65552 | tf_op jit(solution)/shard_map/reduce_scatter | solution.py:71
  250.7 1.7 convolution_bitcast_fusion.5
  252.4 13.9 %psum.30 = f32[128]{0:T(128)S(1)} all-reduce(f32[128]{0:T(128)S(1)} %get-tuple-element.8), channel_id=1, replica_groups=mesh['dom'=64,'rep'=8] {'rep'}, use_global_device_ids=true, to_apply=%region_9.10 | all-reduce | flops 128 | bytes 1024 | tf_op jit(solution)/shard_map/psum | solution.py:78
  266.3 117.4 %psum.31 = f32[128]{0:T(128)} all-reduce(f32[128]{0:T(128)S(1)} %psum.30), channel_id=1, replica_groups=mesh['dom'=64,'rep'=8] {'dom'}, use_global_device_ids=true, to_apply=%region_10.11 | all-reduce | flops 128 | bytes 1024 | tf_op jit(solution)/shard_map/psum | solution.py:78
  385.4 270.4 %all-reduce.5.cloned.1.call-done = f32[128,128]{0,1:T(8,128)} async-done(((f32[128,128]{0,1:T(8,128)}), f32[128,128]{0,1:T(8,128)}) %all-reduce.5.cloned.1.call-update) | async-done | bytes 65552 | tf_op jit(solution)/shard_map/psum | solution.py:78
  (43 shorter events, 14.3 us)
Async XLA Ops:
  7.2 0.8 copy-start
  7.2 243.5 %reduce-scatter.2.cloned.1.call-start = ((), (), s32[]{:S(2)}) async-start(), calls=%async_computation.1 | async-start | bytes 589824 | tf_op jit(solution)/shard_map/reduce_scatter | solution.py:71
  28.3 24.9 %collective-permute-start.3 = (bf16[1024,128]{1,0:T(8,128)(2,1)S(1)}, bf16[1024,128]{1,0:T(8,128)(2,1)S(1)}, u32[]{:S(2)}, u32[]{:S(2)}) collective-permute-start(bf16[1024,128]{1,0:T(8,128)(2,1)S(1)} %all_gather.3), channel_id=1, source_target_pairs={{0,32},{8,40},{16,48},{24,56},{32,0},{40,8},{48,16},{56,24},{64,96... | collective-permute-start | bytes 786440 | tf_op jit(solution)/shard_map/ppermute | solution.py:10
  30.2 33.4 %collective-permute-start.2 = (bf16[1024,128]{1,0:T(8,128)(2,1)S(1)}, bf16[1024,128]{1,0:T(8,128)(2,1)S(1)}, u32[]{:S(2)}, u32[]{:S(2)}) collective-permute-start(bf16[1024,128]{1,0:T(8,128)(2,1)S(1)} %all_gather.3), channel_id=1, source_target_pairs={{0,64},{8,72},{16,80},{24,88},{32,96},{40,104},{48,112},{56,120},{... | collective-permute-start | bytes 786440 | tf_op jit(solution)/shard_map/ppermute | solution.py:10
  32.2 53.7 %collective-permute-start.1 = (bf16[1024,128]{1,0:T(8,128)(2,1)S(1)}, bf16[1024,128]{1,0:T(8,128)(2,1)S(1)}, u32[]{:S(2)}, u32[]{:S(2)}) collective-permute-start(bf16[1024,128]{1,0:T(8,128)(2,1)S(1)} %all_gather.3), channel_id=1, source_target_pairs={{0,128},{8,136},{16,144},{24,152},{32,160},{40,168},{48,176},{56,1... | collective-permute-start | bytes 786440 | tf_op jit(solution)/shard_map/ppermute | solution.py:10
  40.6 47.7 %collective-permute-start = (bf16[1024,128]{1,0:T(8,128)(2,1)S(1)}, bf16[1024,128]{1,0:T(8,128)(2,1)S(1)}, u32[]{:S(2)}, u32[]{:S(2)}) collective-permute-start(bf16[1024,128]{1,0:T(8,128)(2,1)S(1)} %all_gather.3), channel_id=1, source_target_pairs={{0,256},{8,264},{16,272},{24,280},{32,288},{40,296},{48,304},{56,3... | collective-permute-start | bytes 786440 | tf_op jit(solution)/shard_map/ppermute | solution.py:10
  86.6 2.4 copy-start.2
  86.6 2.4 copy-start.3
  107.6 45.0 %collective-permute-start.4 = (f32[1024,128]{1,0:T(8,128)S(1)}, f32[1024,128]{1,0:T(8,128)}, u32[]{:S(2)}, u32[]{:S(2)}) collective-permute-start(f32[1024,128]{1,0:T(8,128)S(1)} %bitcast.141), channel_id=1, source_target_pairs={{0,256},{8,264},{16,272},{24,280},{32,288},{40,296},{48,304},{56,3... | collective-permute-start | bytes 1572872 | tf_op jit(solution)/shard_map/ppermute | solution.py:10
  123.5 80.7 %collective-permute-start.5 = (f32[1024,128]{1,0:T(8,128)S(1)}, f32[1024,128]{1,0:T(8,128)}, u32[]{:S(2)}, u32[]{:S(2)}) collective-permute-start(f32[1024,128]{1,0:T(8,128)S(1)} %bitcast.142), channel_id=1, source_target_pairs={{0,128},{8,136},{16,144},{24,152},{32,160},{40,168},{48,176},{56,1... | collective-permute-start | bytes 1572872 | tf_op jit(solution)/shard_map/ppermute | solution.py:10
  128.1 76.1 %collective-permute-start.6 = (f32[1024,128]{1,0:T(8,128)S(1)}, f32[1024,128]{1,0:T(8,128)S(1)}, u32[]{:S(2)}, u32[]{:S(2)}) collective-permute-start(f32[1024,128]{1,0:T(8,128)S(1)} %bitcast.143), channel_id=1, source_target_pairs={{0,64},{8,72},{16,80},{24,88},{32,96},{40,104},{48,112},{56,120},{... | collective-permute-start | bytes 1572872 | tf_op jit(solution)/shard_map/ppermute | solution.py:10
  134.7 69.5 %collective-permute-start.7 = (f32[1024,128]{1,0:T(8,128)S(1)}, f32[1024,128]{1,0:T(8,128)}, u32[]{:S(2)}, u32[]{:S(2)}) collective-permute-start(f32[1024,128]{1,0:T(8,128)S(1)} %bitcast.144), channel_id=1, source_target_pairs={{0,32},{8,40},{16,48},{24,56},{32,0},{40,8},{48,16},{56,24},{64,96... | collective-permute-start | bytes 1572872 | tf_op jit(solution)/shard_map/ppermute | solution.py:10
  144.4 239.3 %copy-start.1 = (bf16[128,128]{1,0:T(8,128)(2,1)S(1)}, bf16[128,128]{1,0:T(8,128)(2,1)}, u32[]{:S(2)}) copy-start(bf16[128,128]{1,0:T(8,128)(2,1)} %param.8) | copy-start | bytes 98308
  206.5 177.2 %all-reduce.3.cloned.1.call-start = ((), (), s32[]{:S(2)}) async-start(), calls=%async_computation.2 | async-start | bytes 131072 | tf_op jit(solution)/shard_map/psum | solution.py:78
  252.4 403.4 %all-reduce.5.cloned.1.call-start = ((), (), s32[]{:S(2)}) async-start(), calls=%async_computation.3 | async-start | bytes 131072 | tf_op jit(solution)/shard_map/psum | solution.py:78
Sparse Core Ops, SparseCore 0:
  206.6 44.0 reduce-scatter.1
  253.6 74.1 all-reduce.2
  383.9 271.9 all-reduce.4
